TPU v7x, 32 devices: a whole 2x2x4 slice. The times are simulated.
32 devices in a mesh: parts: 2 (over x), elec: 4 (over y, core), walk: 4 (over z).
Axes of the slice: x: 2, y: 2, z: 4, core: 2. Of those that a mesh axis runs over, the one named last changes fastest.
Arguments:
- elec_pos: float32 [3, 32, 512], P(None, ('parts', 'walk'), 'elec'), parts along dimension 1, may hold values from -8 to 8
- atom_pos: float32 [200, 3], P(('parts', 'elec')), parts along dimension 0, may hold values from -8 to 8
- atom_emb: float32 [200, 256], P(('parts', 'elec')), parts along dimension 0, may hold values from -6 to 6
- spin_emb: float32 [2, 256], replicated, may hold values from -6 to 6
- spin: int32 [1024], P(('parts', 'elec')), parts along dimension 0, may hold values from 0 to 1, as said below
- near_atoms: int32 [16, 2], P('parts'), parts along dimension 0, may hold values from 0 to 3
- pair_list: int32 [16, 4], P('parts'), parts along dimension 0, may hold values from 0 to 7, as said below
- pair_count: int32 [16], P('parts'), parts along dimension 0, may hold values from 1 to 4, as said below
- w_query: bfloat16 [256, 256], replicated, may hold values from -64 to 64
- w_key: bfloat16 [256, 256], replicated, may hold values from -0.375 to 0.375
- w_value: bfloat16 [256, 256], replicated, may hold values from -0.375 to 0.375
- w_out: bfloat16 [256, 256], replicated, may hold values from -0.375 to 0.375
- w_orb: bfloat16 [2, 256, 1024], replicated, may hold values from -0.375 to 0.375
- target: bfloat16 [32, 512, 1024], P(('parts', 'walk'), 'elec'), parts along dimension 0, may hold values from -6 to 6
Outputs:
- grad_orb: float32 [4, 256, 1024], P('parts'), parts along dimension 0
- grad_out: float32 [512, 256], P('parts'), parts along dimension 0
- loss: float32 [2], P('parts'), parts along dimension 0
There are 2 independent parts, one for each index of `parts`. A program takes and returns all parts, laid end to end along the dimension named above; an argument that names none is the same for every part. Nothing has to cross between parts.
Inputs may be any that keep to these rules, and one draw needn't show every extreme that they name: `pair_list`: row b lists 4 distinct blocks, the first being b itself; every listed c has c // 2 equal to b // 2 or one more or one less than it, modulo 8 / 2. Only the first pair_count[b] entries of row b are listed; some block lists all 4. Each aligned run of 128 electrons holds exactly half of each spin.
All inputs are finite; a program needn't handle non-finite values.
Results may differ from a plain program's by a relative error of at most 0.002.
Values may be sent and summed in bfloat16 or wider, within the bound.
A program may use at most 64 MiB of HBM per device.

v0:
```python
import math
import jax
import jax.numpy as jnp
from jax import lax
from jax.sharding import PartitionSpec as P

HEADS = 16
BLOCK = 64
ATOM_DEV = 25
NEAR = 2
KMAX = 4


def shifted(block, axis, distance):
    devices = range(lax.axis_size(axis))
    route = [((i - distance) % len(devices), i) for i in devices]
    return lax.ppermute(block, axis, route)


def local(
    elec_pos,
    atom_pos,
    atom_emb,
    spin_emb,
    spin,
    near_atoms,
    pair_list,
    pair_count,
    w_query,
    w_key,
    w_value,
    w_out,
    w_orb,
    target,
):
    walkers = elec_pos.shape[1]
    local_rows = elec_pos.shape[2]
    per_device = local_rows // BLOCK
    elec_count = lax.axis_size("elec")
    elec_index = lax.axis_index("elec")
    model_width = w_query.shape[0]
    head_size = model_width // HEADS
    orbital_count = w_orb.shape[2]
    row_local = walkers * local_rows
    half_rows = local_rows // 2
    all_pos, all_emb = (
        lax.all_gather(atom_pos, "elec", axis=0, tiled=True),
        lax.all_gather(atom_emb, "elec", axis=0, tiled=True),
    )
    my_blocks = elec_index * per_device + jnp.arange(per_device)
    near_here = jnp.take(near_atoms, my_blocks, axis=0)
    near_pos = jnp.take(all_pos.reshape(elec_count, ATOM_DEV, 3), near_here, axis=0).reshape(
        per_device, NEAR * ATOM_DEV, 3
    )
    near_emb = jnp.take(
        all_emb.reshape(elec_count, ATOM_DEV, model_width), near_here, axis=0
    ).reshape(per_device, NEAR * ATOM_DEV, model_width)
    positions = elec_pos.reshape(3, walkers, per_device, BLOCK)
    distance = jnp.zeros((walkers, per_device, BLOCK, NEAR * ATOM_DEV), jnp.float32)
    for axis_id in range(3):
        spacing = positions[axis_id][..., None] - near_pos[None, :, None, :, axis_id]
        distance = distance + spacing * spacing
    closeness = 1.0 / (1.0 + distance)
    atom_term = jnp.einsum(
        "wbea,bad->wbed", closeness, near_emb, precision=lax.Precision.HIGHEST
    ).reshape(walkers, local_rows, model_width)
    spin_rows = jnp.where(spin[:, None] == 1, spin_emb[1][None, :], spin_emb[0][None, :])
    hidden = (atom_term + spin_rows[None]).astype(jnp.bfloat16)
    flat_rows = hidden.reshape(row_local, model_width)
    queries = (
        jnp.dot(flat_rows, w_query, preferred_element_type=jnp.float32)
        .astype(jnp.bfloat16)
        .reshape(walkers, local_rows, HEADS, head_size)
    )
    key_rows = (
        jnp.dot(flat_rows, w_key, preferred_element_type=jnp.float32)
        .astype(jnp.bfloat16)
        .reshape(walkers, local_rows, model_width)
    )
    value_rows = (
        jnp.dot(flat_rows, w_value, preferred_element_type=jnp.float32)
        .astype(jnp.bfloat16)
        .reshape(walkers, local_rows, model_width)
    )
    block_count = elec_count * per_device
    lists_here = jnp.take(pair_list, my_blocks, axis=0)
    counts_here = jnp.take(pair_count, my_blocks, axis=0)
    slot_ids = jnp.arange(KMAX)
    in_list = slot_ids[None, :] < counts_here[:, None]
    listed = jnp.any(
        (lists_here[:, :, None] == jnp.arange(block_count)[None, None, :]) & in_list[:, :, None],
        axis=1,
    )
    score_scale = 1.0 / math.sqrt(head_size)

    def attend_piece(running, key_part, value_part, key_blocks):
        old_max, old_total, old_acc = running
        key_count = key_part.shape[1]
        allowed = jnp.repeat(jnp.take(listed, key_blocks, axis=1), BLOCK, axis=0)
        key_mask = allowed[None, :, None, :]
        key_heads = key_part.reshape(walkers, key_count, HEADS, head_size)
        value_heads = value_part.reshape(walkers, key_count, HEADS, head_size)
        scores = (
            jnp.einsum("wqhd,wkhd->wqhk", queries, key_heads, preferred_element_type=jnp.float32)
            * score_scale
        )
        scores = jnp.where(key_mask, scores, -1e30)
        new_max = jnp.maximum(old_max, jnp.max(scores, axis=3))
        weights = jnp.where(key_mask, jnp.exp(scores - new_max[..., None]), 0.0)
        factor = jnp.exp(old_max - new_max)
        new_total = old_total * factor + jnp.sum(weights, axis=3)
        new_acc = old_acc * factor[..., None] + jnp.einsum(
            "wqhk,wkhd->wqhd",
            weights.astype(jnp.bfloat16),
            value_heads,
            preferred_element_type=jnp.float32,
        )
        return (new_max, new_total, new_acc)

    def shard_blocks(owner):
        return (owner * local_rows + jnp.arange(local_rows)) // BLOCK

    lower_owner = (elec_index + elec_count - 1) % elec_count
    upper_owner = (elec_index + 1) % elec_count
    initial = (
        jnp.full((walkers, local_rows, HEADS), -1e30, jnp.float32),
        jnp.zeros((walkers, local_rows, HEADS), jnp.float32),
        jnp.zeros((walkers, local_rows, HEADS, head_size), jnp.float32),
    )
    lower_kv = shifted((key_rows, value_rows), "elec", 1)
    upper_kv = shifted((key_rows, value_rows), "elec", -1)
    running = attend_piece(initial, key_rows, value_rows, shard_blocks(elec_index))
    running = attend_piece(running, lower_kv[0], lower_kv[1], shard_blocks(lower_owner))
    running = attend_piece(running, upper_kv[0], upper_kv[1], shard_blocks(upper_owner))
    final_max, final_total, final_acc = running
    attended = (
        (final_acc / final_total[..., None]).astype(jnp.bfloat16).reshape(row_local, model_width)
    )
    mixed_out = jnp.dot(attended, w_out, preferred_element_type=jnp.float32)
    hidden_out = (flat_rows.astype(jnp.float32) + mixed_out).astype(jnp.bfloat16)
    by_spin = jnp.argsort(spin, stable=True)
    sorted_hidden = jnp.take(hidden_out.reshape(walkers, local_rows, model_width), by_spin, axis=1)
    sorted_attended = jnp.take(attended.reshape(walkers, local_rows, model_width), by_spin, axis=1)
    sorted_target = jnp.take(target, by_spin, axis=1)
    loss_part = jnp.float32(0.0)
    orb_terms = []
    out_part = jnp.zeros((model_width, model_width), jnp.float32)
    for spin_id in range(2):
        hidden_group = sorted_hidden[:, spin_id * half_rows : (spin_id + 1) * half_rows].reshape(
            walkers * half_rows, model_width
        )
        attended_group = sorted_attended[
            :, spin_id * half_rows : (spin_id + 1) * half_rows
        ].reshape(walkers * half_rows, model_width)
        target_group = sorted_target[:, spin_id * half_rows : (spin_id + 1) * half_rows].reshape(
            walkers * half_rows, orbital_count
        )
        orbitals = jnp.dot(hidden_group, w_orb[spin_id], preferred_element_type=jnp.float32)
        residual = orbitals - target_group.astype(jnp.float32)
        loss_part = loss_part + 0.5 * jnp.sum(residual * residual)
        signal = residual.astype(jnp.bfloat16)
        orb_terms.append(
            lax.dot_general(
                hidden_group, signal, (((0,), (0,)), ((), ())), preferred_element_type=jnp.float32
            )
        )
        backward = lax.dot_general(
            signal, w_orb[spin_id], (((1,), (1,)), ((), ())), preferred_element_type=jnp.float32
        ).astype(jnp.bfloat16)
        out_part = out_part + lax.dot_general(
            attended_group, backward, (((0,), (0,)), ((), ())), preferred_element_type=jnp.float32
        )
    orb_part = jnp.stack(orb_terms, axis=0)
    orb_sum, out_sum, loss_sum = lax.psum((orb_part, out_part, loss_part), ("elec", "walk"))
    rows_float = jnp.float32(row_local * elec_count * lax.axis_size("walk"))
    grad_orb = orb_sum / rows_float
    grad_out = out_sum / rows_float
    loss = jnp.reshape(loss_sum / rows_float, (1,))
    return (grad_orb, grad_out, loss)


def solution(mesh):
    in_specs = (
        P(None, ("parts", "walk"), "elec"),
        P(("parts", "elec"), None),
        P(("parts", "elec"), None),
        P(),
        P(("parts", "elec")),
        P("parts", None),
        P("parts", None),
        P("parts"),
        P(),
        P(),
        P(),
        P(),
        P(),
        P(("parts", "walk"), "elec", None),
    )
    out_specs = (P("parts", None, None), P("parts", None), P("parts"))
    return jax.shard_map(local, mesh=mesh, in_specs=in_specs, out_specs=out_specs, check_vma=False)
```

profile of v0, /device:TPU:0, one launch (start us, length us, event | category | flops | bytes accessed | tf_op | source)
XLA Modules:
  0.0 197.2 jit_solution(5505594694340146671)
XLA Ops:
  9.0 6.3 %all-gather.1 = f32[4,25,3]{1,2,0:T(4,128)S(1)} all-gather(f32[1,25,3]{1,2,0:T(4,128)} %bitcast.217), channel_id=1, replica_groups=mesh['parts'=2,'elec'=4,'walk'=4] {'elec'}, dimensions={0}, use_global_device_ids=true | all-gather | bytes 1500 | tf_op jit(solution)/shard_map/all_gather | solution.py:47
  16.1 5.8 %all-gather = f32[4,25,256]{2,1,0:T(8,128)S(1)} all-gather(f32[1,25,256]{2,1,0:T(8,128)} %bitcast.214), channel_id=1, replica_groups=mesh['parts'=2,'elec'=4,'walk'=4] {'elec'}, dimensions={0}, use_global_device_ids=true | all-gather | bytes 128000 | tf_op jit(solution)/shard_map/all_gather | solution.py:48
  26.6 1.4 collective-permute-start.2
  29.3 2.5 %sort.17 = (s32[128]{0:T(128)}, s32[128]{0:T(128)S(1)}) sort(s32[128]{0:T(128)S(1)} %copy-done.14, s32[128]{0:T(128)S(1)} %iota.37), dimensions={0}, to_apply=%region_7.9 | sort | flops 896 | bytes 2048 | tf_op jit(solution)/shard_map/jit(argsort)/sort | solution.py:141
  37.9 3.7 %gather_fusion.5 = bf16[128,4,1024]{2,0,1:T(8,128)(2,1)S(1)} fusion(bf16[4,128,1024]{2,1,0:T(8,128)(2,1)S(1)} %copy-done, s32[1024]{0:T(1024)S(1)} %pad_clamp_fusion), kind=kCustom, calls=%fused_computation.10 | custom fusion | bytes 2097664 | tf_op jit(solution)/shard_map/jit(_take)/gather | solution.py:144
  41.7 2.9 %fusion = (f32[4,128,16]{1,2,0:T(8,128)S(1)}, f32[4,16,128,128]{3,2,1,0:T(8,128)}) fusion(pred[128,128]{0,1:T(8,128)(4,1)S(1)} %copy.146, bf16[4,128,16,16]{1,0,3,2:T(4,128)(2,1)S(1)} %reshape.316, bf16[4,128,16,16]{1,0,3,2:T(4,128)(2,1)S(1)} %reshape_reshape.9), kind=kOutput, calls=%fused_computation.17 | convolution fusion | flops 36691968 | bytes 4767744 | tf_op jit(solution)/shard_map/wqhd,wkhd->wqhk/dot_general | solution.py:104
  44.6 1.1 fusion.117
  45.7 1.1 copy.157
  46.9 2.8 %fusion.1 = (f32[4,128,16]{1,2,0:T(8,128)S(1)}, f32[4,16,128,128]{3,2,1,0:T(8,128)}) fusion(pred[128,128]{0,1:T(8,128)(4,1)S(1)} %copy.156, bf16[4,128,16,16]{1,3,2,0:T(8,128)(2,1)S(1)} %bitcast.193, bf16[4,128,16,16]{1,0,3,2:T(4,128)(2,1)S(1)} %reshape.316), kind=kOutput, calls=%fused_computation.18 | convolution fusion | flops 36691968 | bytes 4767744 | tf_op jit(solution)/shard_map/wqhd,wkhd->wqhk/dot_general | solution.py:104
  51.8 1.3 fusion.7
  53.7 2.1 %copy-done.3 = f32[4,16,128,128]{3,2,1,0:T(8,128)S(1)} copy-done((f32[4,16,128,128]{3,2,1,0:T(8,128)S(1)}, f32[4,16,128,128]{3,2,1,0:T(8,128)}, u32[]{:S(2)}) %copy-start.3) | copy-done | bytes 4194328
  55.8 2.3 %fusion.3 = (f32[4,128,16]{1,2,0:T(8,128)S(1)}, f32[4,128,16]{1,2,0:T(8,128)S(1)}) fusion(f32[4,16,128,128]{3,2,1,0:T(8,128)S(1)} %copy-done.3, f32[4,128,16]{1,2,0:T(8,128)S(1)} %get-tuple-element.21, pred[128,128]{0,1:T(8,128)(4,1)S(1)} %copy.146, f32[4,128,16]{1,2,0:T(8,128)S(1)} %get-tuple-element.13, f32[4,16,128,128]{3,2,1,0:T(8,128)S(1)} %copy-done.2, ...), kind=kLoop, calls=%fused_computation.20 | loop fusion | flops 10469376 | bytes 8552448 | tf_op jit(solution)/shard_map/reduce_sum | solution.py:111
  58.2 1.8 fusion.33
  61.1 3.1 %fusion.24 = f32[4,128,16,16]{1,3,2,0:T(8,128)S(1)} fusion(bf16[4,128,16,16]{1,3,2,0:T(8,128)(2,1)S(1)} %bitcast.207, f32[4,16,128,128]{3,2,1,0:T(8,128)} %copy-done.4, f32[4,128,16]{1,2,0:T(8,128)S(1)} %get-tuple-element.12, pred[128,128]{0,1:T(8,128)(4,1)S(1)} %copy.163), kind=kOutput, calls=%fused_computation.39 | convolution fusion | flops 38797312 | bytes 5029888 | tf_op jit(solution)/shard_map/wqhk,wkhd->wqhd/dot_general | solution.py:112
  64.2 1.1 copy.159
  65.3 3.3 %fusion.47 = bf16[4,128,16,16]{1,3,2,0:T(8,128)(2,1)S(1)} fusion(f32[4,128,16,16]{1,3,2,0:T(8,128)S(1)} %fusion.24, f32[4,128,16,16]{1,3,2,0:T(8,128)} %fusion.33, bf16[4,128,16,16]{1,3,2,0:T(8,128)(2,1)S(1)} %bitcast.206, f32[4,16,128,128]{3,2,1,0:T(8,128)} %get-tuple-element.35, f32[4,128,16]{1,2,0:T(8,128)S(1)} %get-tuple-element.13, ...), kind=kOutput, calls=%fused_computation.60 | convolution fusion | flops 39452672 | bytes 5881856 | tf_op jit(solution)/shard_map/wqhk,wkhd->wqhd/dot_general | solution.py:112
  71.9 2.2 %multiply_reduce_fusion.1 = (f32[]{:T(128)}, bf16[256,1024]{1,0:T(8,128)(2,1)S(1)}) fusion(bf16[256,1024]{1,0:T(8,128)(2,1)} %bitcast.200, bf16[256,256]{1,0:T(8,128)(2,1)S(1)} %bitcast.203, bf16[2,256,1024]{2,1,0:T(8,128)(2,1)} %param.30), kind=kOutput, calls=%fused_computation.57 | convolution fusion | flops 135528448 | bytes 1703940 | tf_op jit(solution)/shard_map/dot_general | solution.py:158
  74.4 2.3 %fusion.43 = f32[256,256]{1,0:T(8,128)} fusion(bf16[256,256]{1,0:T(8,128)(2,1)S(1)} %bitcast.210, bf16[2,256,1024]{2,1,0:T(8,128)(2,1)} %param.30, bf16[256,1024]{1,0:T(8,128)(2,1)S(1)} %get-tuple-element.39), kind=kOutput, calls=%fused_computation.54 | convolution fusion | flops 167837696 | bytes 1441792 | tf_op jit(solution)/shard_map/dot_general | solution.py:170
  76.8 2.1 %multiply_reduce_fusion = (f32[]{:T(128)}, bf16[256,1024]{1,0:T(8,128)(2,1)S(1)}) fusion(bf16[256,1024]{1,0:T(8,128)(2,1)S(1)} %bitcast.199, bf16[256,256]{1,0:T(8,128)(2,1)S(1)} %bitcast.201, bf16[2,256,1024]{2,1,0:T(8,128)(2,1)} %param.30), kind=kOutput, calls=%fused_computation.56 | convolution fusion | flops 135528448 | bytes 1703940 | tf_op jit(solution)/shard_map/dot_general | solution.py:158
  80.0 2.5 %convolution_add_fusion.1 = f32[256,256]{1,0:T(8,128)} fusion(f32[256,256]{1,0:T(8,128)} %fusion.43, bf16[256,256]{1,0:T(8,128)(2,1)S(1)} %bitcast.205, bf16[2,256,1024]{2,1,0:T(8,128)(2,1)} %param.30, bf16[256,1024]{1,0:T(8,128)(2,1)} %copy-done.5), kind=kOutput, calls=%fused_computation.51 | convolution fusion | flops 167903232 | bytes 1703936 | tf_op jit(solution)/shard_map/dot_general | solution.py:170
  82.5 1.5 pad_maximum_fusion
  85.2 35.5 %psum.23 = f32[]{:T(128)} all-reduce(f32[]{:T(128)S(6)} %add.215), channel_id=1, replica_groups=mesh['parts'=2,'elec'=4,'walk'=4] {'elec','walk'}, use_global_device_ids=true, to_apply=%region_12.15 | all-reduce | flops 1 | bytes 8 | tf_op jit(solution)/shard_map/psum | solution.py:174
  121.4 63.9 %all-reduce.3.cloned.1.call-done = (f32[2,256,1024]{2,1,0:T(8,128)}, f32[256,256]{1,0:T(8,128)}) async-done(((f32[2,256,1024]{2,1,0:T(8,128)}, f32[256,256]{1,0:T(8,128)}), (f32[2,256,1024]{2,1,0:T(8,128)}, f32[256,256]{1,0:T(8,128)})) %all-reduce.3.cloned.1.call-update) | async-done | bytes 2359312 | tf_op jit(solution)/shard_map/psum | solution.py:174
  185.2 3.3 %broadcast_multiply_fusion = f32[2,256,1024]{2,1,0:T(8,128)} fusion(f32[2,256,1024]{2,1,0:T(8,128)} %get-tuple-element.7), kind=kLoop, calls=%fused_computation.58 | loop fusion | flops 524288 | bytes 4194304 | tf_op jit(solution)/shard_map/div | solution.py:176
  (136 shorter events, 23.5 us)
Async XLA Ops:
  7.2 30.7 %copy-start = (bf16[4,128,1024]{2,1,0:T(8,128)(2,1)S(1)}, bf16[4,128,1024]{2,1,0:T(8,128)(2,1)}, u32[]{:S(2)}) copy-start(bf16[4,128,1024]{2,1,0:T(8,128)(2,1)} %param.31) | copy-start | bytes 3145732
  7.2 22.1 %copy-start.14 = (s32[128]{0:T(128)S(1)}, s32[128]{0:T(128)}, u32[]{:S(2)}) copy-start(s32[128]{0:T(128)} %param.22) | copy-start | bytes 1540
  7.2 18.8 %copy-start.9 = (bf16[256,256]{1,0:T(8,128)(2,1)S(1)}, bf16[256,256]{1,0:T(8,128)(2,1)}, u32[]{:S(2)}) copy-start(bf16[256,256]{1,0:T(8,128)(2,1)} %param.27) | copy-start | bytes 393220
  7.2 20.8 %copy-start.10 = (bf16[256,256]{1,0:T(8,128)(2,1)S(1)}, bf16[256,256]{1,0:T(8,128)(2,1)}, u32[]{:S(2)}) copy-start(bf16[256,256]{1,0:T(8,128)(2,1)} %param.28) | copy-start | bytes 393220
  7.2 24.6 %copy-start.12 = (s32[8,4]{0,1:T(4,128)S(1)}, s32[8,4]{0,1:T(4,128)}, u32[]{:S(2)}) copy-start(s32[8,4]{0,1:T(4,128)} %param.24) | copy-start | bytes 388
  7.2 25.3 %copy-start.1 = (s32[8]{0:T(128)S(1)}, s32[8]{0:T(128)}, u32[]{:S(2)}) copy-start(s32[8]{0:T(128)} %param.25) | copy-start | bytes 100
  7.2 27.3 %copy-start.11 = (bf16[256,256]{1,0:T(8,128)(2,1)S(1)}, bf16[256,256]{1,0:T(8,128)(2,1)}, u32[]{:S(2)}) copy-start(bf16[256,256]{1,0:T(8,128)(2,1)} %param.26) | copy-start | bytes 393220
  7.2 178.0 %all-reduce.3.cloned.1.call-start = ((), (), s32[]{:S(2)}) async-start(), calls=%async_computation | async-start | bytes 4718592 | tf_op jit(solution)/shard_map/psum | solution.py:174
  26.2 19.6 %collective-permute-start = (bf16[4,128,256]{2,1,0:T(8,128)(2,1)S(1)}, bf16[4,128,256]{2,1,0:T(8,128)(2,1)}, u32[]{:S(2)}, u32[]{:S(2)}) collective-permute-start(bf16[4,128,256]{2,1,0:T(8,128)(2,1)S(1)} %bitcast.196), channel_id=1, source_target_pairs={{12,0},{0,4},{4,8},{8,12},{13,1},{1,5},{5,9},{9,13},{14,2},{2,6},{... | collective-permute-start | bytes 786440 | tf_op jit(solution)/shard_map/ppermute | solution.py:17
  26.6 23.1 %collective-permute-start.2 = (bf16[4,128,256]{2,1,0:T(8,128)(2,1)S(1)}, bf16[4,128,256]{2,1,0:T(8,128)(2,1)}, u32[]{:S(2)}, u32[]{:S(2)}) collective-permute-start(bf16[4,128,256]{2,1,0:T(8,128)(2,1)S(1)} %bitcast.197), channel_id=1, source_target_pairs={{4,0},{8,4},{12,8},{0,12},{5,1},{9,5},{13,9},{1,13},{6,2},{10,6},{... | collective-permute-start | bytes 786440 | tf_op jit(solution)/shard_map/ppermute | solution.py:17
  28.3 31.7 %collective-permute-start.3 = (bf16[4,128,256]{2,1,0:T(8,128)(2,1)S(1)}, bf16[4,128,256]{2,1,0:T(8,128)(2,1)}, u32[]{:S(2)}, u32[]{:S(2)}) collective-permute-start(bf16[4,128,256]{2,1,0:T(8,128)(2,1)S(1)} %bitcast.194), channel_id=1, source_target_pairs={{4,0},{8,4},{12,8},{0,12},{5,1},{9,5},{13,9},{1,13},{6,2},{10,6},{... | collective-permute-start | bytes 786440 | tf_op jit(solution)/shard_map/ppermute | solution.py:17
  28.7 35.4 %collective-permute-start.1 = (bf16[4,128,256]{2,1,0:T(8,128)(2,1)S(1)}, bf16[4,128,256]{2,1,0:T(8,128)(2,1)}, u32[]{:S(2)}, u32[]{:S(2)}) collective-permute-start(bf16[4,128,256]{2,1,0:T(8,128)(2,1)S(1)} %bitcast.195), channel_id=1, source_target_pairs={{12,0},{0,4},{4,8},{8,12},{13,1},{1,5},{5,9},{9,13},{14,2},{2,6},{... | collective-permute-start | bytes 786440 | tf_op jit(solution)/shard_map/ppermute | solution.py:17
  50.8 2.9 %copy-start.2 = (f32[4,16,128,128]{3,2,1,0:T(8,128)S(1)}, f32[4,16,128,128]{3,2,1,0:T(8,128)}, u32[]{:S(2)}) copy-start(f32[4,16,128,128]{3,2,1,0:T(8,128)} %get-tuple-element.35) | copy-start | bytes 12582916
  50.8 5.0 %copy-start.3 = (f32[4,16,128,128]{3,2,1,0:T(8,128)S(1)}, f32[4,16,128,128]{3,2,1,0:T(8,128)}, u32[]{:S(2)}) copy-start(f32[4,16,128,128]{3,2,1,0:T(8,128)} %get-tuple-element.37) | copy-start | bytes 12582916
  51.8 6.3 %copy-start.4 = (f32[4,16,128,128]{3,2,1,0:T(8,128)}, f32[4,16,128,128]{3,2,1,0:T(8,128)S(1)}, u32[]{:S(2)}) copy-start(f32[4,16,128,128]{3,2,1,0:T(8,128)S(1)} %get-tuple-element.33) | copy-start | bytes 12582916
  55.8 2.3 %copy-start.7 = (bf16[4,128,16,16]{1,0,3,2:T(4,128)(2,1)S(1)}, bf16[4,128,16,16]{1,0,3,2:T(4,128)(2,1)}, u32[]{:S(2)}) copy-start(bf16[4,128,16,16]{1,0,3,2:T(4,128)(2,1)} %reshape_reshape.10) | copy-start | bytes 786436
  65.3 3.6 %copy-start.13 = (bf16[256,256]{1,0:T(8,128)(2,1)S(1)}, bf16[256,256]{1,0:T(8,128)(2,1)}, u32[]{:S(2)}) copy-start(bf16[256,256]{1,0:T(8,128)(2,1)} %param.29) | copy-start | bytes 393220
  71.2 5.5 %copy-start.6 = (bf16[4,64,1024]{2,1,0:T(8,128)(2,1)S(1)}, bf16[4,64,1024]{2,1,0:T(8,128)(2,1)}, u32[]{:S(2)}) copy-start(bf16[4,64,1024]{2,1,0:T(8,128)(2,1)} %get-tuple-element.15) | copy-start | bytes 1572868
  78.8 0.8 copy-start.5
  185.2 3.3 %copy-start.8 = (f32[256,256]{1,0:T(8,128)S(1)}, f32[256,256]{1,0:T(8,128)}, u32[]{:S(2)}) copy-start(f32[256,256]{1,0:T(8,128)} %get-tuple-element.8) | copy-start | bytes 786436
Sparse Core Ops, SparseCore 0:
  84.1 101.0 all-reduce.2
where the time goes:
time: 198 us; the launch traced here: 197 us
  waiting for transfers between devices  63.9 us (32%)
  blocking collectives  47.7 us (24%)
  matrix products  26.4 us (13%)
  local copies, waits for them, and re-layouts  25.5 us (13%)
  between operations  17.6 us (9%)
  other arithmetic  13.7 us (7%)
  starting transfers between devices  2.44 us (1%)
    psum x1, waiting for transfers between devices, local(): lax.psum((orb_part, out_part, loss_part), ('elec', 'walk'))  63.9 us
    psum x1, blocking collectives, local(): lax.psum((orb_part, out_part, loss_part), ('elec', 'walk'))  35.5 us
    dot_general x3, matrix products, attend_piece(): jnp.einsum('wqhk,wkhd->wqhd', weights.astype(jnp.bfloat16), value_heads,...  8.22 us
    dot_general x3, matrix products, attend_piece(): jnp.einsum('wqhd,wkhd->wqhk', queries, key_heads, preferred_element_type=...  6.68 us
    all_gather x1, blocking collectives, local(): lax.all_gather(atom_pos, 'elec', axis=0, tiled=True)  6.28 us
    all_gather x1, blocking collectives, local(): lax.all_gather(atom_emb, 'elec', axis=0, tiled=True)  5.85 us
    dot_general x2, matrix products, local(): lax.dot_general(attended_group, backward, (((0,), (0,)), ((), ())), prefe...  4.87 us
    unnamed x32, local copies, waits for them, and re-layouts  4.51 us
  transfers between devices with their start and end apart: 5, of which 1 were waited for; matrix products, arithmetic and copies ran while one was open for 16% of the time, Pallas kernels for 0%

commit v1 on v0

--- a/solution.py
+++ b/solution.py
@@ -171,7 +171,9 @@
             attended_group, backward, (((0,), (0,)), ((), ())), preferred_element_type=jnp.float32
         )
     orb_part = jnp.stack(orb_terms, axis=0)
-    orb_sum, out_sum, loss_sum = lax.psum((orb_part, out_part, loss_part), ("elec", "walk"))
+    orb_sum, out_sum, loss_sum = lax.psum(
+        lax.psum((orb_part, out_part, loss_part), axis_name="walk"), axis_name="elec"
+    )
     rows_float = jnp.float32(row_local * elec_count * lax.axis_size("walk"))
     grad_orb = orb_sum / rows_float
     grad_out = out_sum / rows_float

time: 198 us -> 252 us (1.27)
  waiting for transfers between devices: 63.9 us -> 136 us
  blocking collectives: 47.7 us -> 29.3 us
    psum x1 -> x2, waiting for transfers between devices: 63.9 us -> 136 us  [the longest x1 97.6 us: local(): lax.psum((orb_part, out_part, loss_part), axis_name='walk')]
    psum x1 -> x2, blocking collectives: 35.5 us -> 17.1 us  [the longest x1 9.98 us: local(): lax.psum((orb_part, out_part, loss_part), axis_name='walk')]
  transfers between devices with their start and end apart: 5 -> 6, of which waited for: 1 -> 2; matrix products, arithmetic and copies ran while one was open for 16% -> 13% of each run, Pallas kernels for 0% -> 0%
where the time goes in v1:
time: 252 us; the launch traced here: 251 us
  waiting for transfers between devices  136 us (54%)
  blocking collectives  29.3 us (12%)
  matrix products  26.4 us (10%)
  local copies, waits for them, and re-layouts  25.5 us (10%)
  between operations  17.6 us (7%)
  other arithmetic  13.7 us (5%)
    psum x1, waiting for transfers between devices, local(): lax.psum((orb_part, out_part, loss_part), axis_name='walk')  97.6 us
    psum x1, waiting for transfers between devices, local(): lax.psum(lax.psum((orb_part, out_part, loss_part), axis_name='walk'), axi...  38.5 us
    psum x1, blocking collectives, local(): lax.psum((orb_part, out_part, loss_part), axis_name='walk')  9.98 us
    dot_general x3, matrix products, attend_piece(): jnp.einsum('wqhk,wkhd->wqhd', weights.astype(jnp.bfloat16), value_heads,...  8.22 us
    psum x1, blocking collectives, local(): lax.psum(lax.psum((orb_part, out_part, loss_part), axis_name='walk'), axi...  7.16 us
    dot_general x3, matrix products, attend_piece(): jnp.einsum('wqhd,wkhd->wqhk', queries, key_heads, preferred_element_type=...  6.68 us
    all_gather x1, blocking collectives, local(): lax.all_gather(atom_pos, 'elec', axis=0, tiled=True)  6.28 us
    all_gather x1, blocking collectives, local(): lax.all_gather(atom_emb, 'elec', axis=0, tiled=True)  5.85 us
  transfers between devices with their start and end apart: 6, of which 2 were waited for; matrix products, arithmetic and copies ran while one was open for 13% of the time, Pallas kernels for 0%

profile of v1, /device:TPU:0, one launch (start us, length us, event | category | flops | bytes accessed | tf_op | source)
XLA Modules:
  0.0 251.1 jit_solution(1149727703964630522)
XLA Ops:
  9.0 6.3 %all-gather.1 = f32[4,25,3]{1,2,0:T(4,128)S(1)} all-gather(f32[1,25,3]{1,2,0:T(4,128)} %bitcast.217), channel_id=1, replica_groups=mesh['parts'=2,'elec'=4,'walk'=4] {'elec'}, dimensions={0}, use_global_device_ids=true | all-gather | bytes 1500 | tf_op jit(solution)/shard_map/all_gather | solution.py:47
  16.1 5.8 %all-gather = f32[4,25,256]{2,1,0:T(8,128)S(1)} all-gather(f32[1,25,256]{2,1,0:T(8,128)} %bitcast.214), channel_id=1, replica_groups=mesh['parts'=2,'elec'=4,'walk'=4] {'elec'}, dimensions={0}, use_global_device_ids=true | all-gather | bytes 128000 | tf_op jit(solution)/shard_map/all_gather | solution.py:48
  26.6 1.4 collective-permute-start.2
  29.3 2.5 %sort.17 = (s32[128]{0:T(128)}, s32[128]{0:T(128)S(1)}) sort(s32[128]{0:T(128)S(1)} %copy-done.14, s32[128]{0:T(128)S(1)} %iota.37), dimensions={0}, to_apply=%region_7.9 | sort | flops 896 | bytes 2048 | tf_op jit(solution)/shard_map/jit(argsort)/sort | solution.py:141
  37.9 3.7 %gather_fusion.5 = bf16[128,4,1024]{2,0,1:T(8,128)(2,1)S(1)} fusion(bf16[4,128,1024]{2,1,0:T(8,128)(2,1)S(1)} %copy-done, s32[1024]{0:T(1024)S(1)} %pad_clamp_fusion), kind=kCustom, calls=%fused_computation.10 | custom fusion | bytes 2097664 | tf_op jit(solution)/shard_map/jit(_take)/gather | solution.py:144
  41.7 2.9 %fusion = (f32[4,128,16]{1,2,0:T(8,128)S(1)}, f32[4,16,128,128]{3,2,1,0:T(8,128)}) fusion(pred[128,128]{0,1:T(8,128)(4,1)S(1)} %copy.146, bf16[4,128,16,16]{1,0,3,2:T(4,128)(2,1)S(1)} %reshape.316, bf16[4,128,16,16]{1,0,3,2:T(4,128)(2,1)S(1)} %reshape_reshape.9), kind=kOutput, calls=%fused_computation.17 | convolution fusion | flops 36691968 | bytes 4767744 | tf_op jit(solution)/shard_map/wqhd,wkhd->wqhk/dot_general | solution.py:104
  46.9 2.8 %fusion.1 = (f32[4,128,16]{1,2,0:T(8,128)S(1)}, f32[4,16,128,128]{3,2,1,0:T(8,128)}) fusion(pred[128,128]{0,1:T(8,128)(4,1)S(1)} %copy.156, bf16[4,128,16,16]{1,3,2,0:T(8,128)(2,1)S(1)} %bitcast.193, bf16[4,128,16,16]{1,0,3,2:T(4,128)(2,1)S(1)} %reshape.316), kind=kOutput, calls=%fused_computation.18 | convolution fusion | flops 36691968 | bytes 4767744 | tf_op jit(solution)/shard_map/wqhd,wkhd->wqhk/dot_general | solution.py:104
  51.8 1.3 fusion.7
  53.7 2.1 copy-done.3
  55.8 2.3 fusion.3
  58.2 1.8 fusion.33
  61.1 3.1 %fusion.24 = f32[4,128,16,16]{1,3,2,0:T(8,128)S(1)} fusion(bf16[4,128,16,16]{1,3,2,0:T(8,128)(2,1)S(1)} %bitcast.207, f32[4,16,128,128]{3,2,1,0:T(8,128)} %copy-done.4, f32[4,128,16]{1,2,0:T(8,128)S(1)} %get-tuple-element.14, pred[128,128]{0,1:T(8,128)(4,1)S(1)} %copy.163), kind=kOutput, calls=%fused_computation.39 | convolution fusion | flops 38797312 | bytes 5029888 | tf_op jit(solution)/shard_map/wqhk,wkhd->wqhd/dot_general | solution.py:112
  64.2 1.1 copy.159
  65.3 3.3 %fusion.47 = bf16[4,128,16,16]{1,3,2,0:T(8,128)(2,1)S(1)} fusion(f32[4,128,16,16]{1,3,2,0:T(8,128)S(1)} %fusion.24, f32[4,128,16,16]{1,3,2,0:T(8,128)} %fusion.33, bf16[4,128,16,16]{1,3,2,0:T(8,128)(2,1)S(1)} %bitcast.206, f32[4,16,128,128]{3,2,1,0:T(8,128)} %get-tuple-element.37, f32[4,128,16]{1,2,0:T(8,128)S(1)} %get-tuple-element.15, ...), kind=kOutput, calls=%fused_computation.60 | convolution fusion | flops 39452672 | bytes 5881856 | tf_op jit(solution)/shard_map/wqhk,wkhd->wqhd/dot_general | solution.py:112
  71.9 2.2 multiply_reduce_fusion.1
  74.4 2.3 fusion.43
  76.7 2.1 multiply_reduce_fusion
  79.9 2.5 %convolution_add_fusion.1 = f32[256,256]{1,0:T(8,128)} fusion(f32[256,256]{1,0:T(8,128)} %fusion.43, bf16[256,256]{1,0:T(8,128)(2,1)S(1)} %bitcast.205, bf16[2,256,1024]{2,1,0:T(8,128)(2,1)} %param.30, bf16[256,1024]{1,0:T(8,128)(2,1)} %copy-done.5), kind=kOutput, calls=%fused_computation.51 | convolution fusion | flops 167903232 | bytes 1703936 | tf_op jit(solution)/shard_map/dot_general | solution.py:170
  82.5 1.5 pad_maximum_fusion
  84.0 97.6 %all-reduce.5.cloned.1.call-done = (f32[2,256,1024]{2,1,0:T(8,128)}, f32[256,256]{1,0:T(8,128)}) async-done(((f32[2,256,1024]{2,1,0:T(8,128)}, f32[256,256]{1,0:T(8,128)}), (f32[2,256,1024]{2,1,0:T(8,128)}, f32[256,256]{1,0:T(8,128)})) %all-reduce.5.cloned.1.call-update) | async-done | bytes 2359312 | tf_op jit(solution)/shard_map/psum | solution.py:175
  182.8 10.0 %psum.46 = f32[]{:T(128)} all-reduce(f32[]{:T(128)S(6)} %add.221), channel_id=1, replica_groups=mesh['parts'=2,'elec'=4,'walk'=4] {'walk'}, use_global_device_ids=true, to_apply=%region_14.17 | all-reduce | flops 1 | bytes 8 | tf_op jit(solution)/shard_map/psum | solution.py:175
  192.8 7.2 %psum.47 = f32[]{:T(128)} all-reduce(f32[]{:T(128)} %psum.46), channel_id=1, replica_groups=mesh['parts'=2,'elec'=4,'walk'=4] {'elec'}, use_global_device_ids=true, to_apply=%region_15.18 | all-reduce | flops 1 | bytes 8 | tf_op jit(solution)/shard_map/psum | solution.py:174
  200.6 38.5 %all-reduce.7.cloned.1.call-done = (f32[2,256,1024]{2,1,0:T(8,128)}, f32[256,256]{1,0:T(8,128)}) async-done(((f32[2,256,1024]{2,1,0:T(8,128)}, f32[256,256]{1,0:T(8,128)}), (f32[2,256,1024]{2,1,0:T(8,128)}, f32[256,256]{1,0:T(8,128)})) %all-reduce.7.cloned.1.call-update) | async-done | bytes 2359312 | tf_op jit(solution)/shard_map/psum | solution.py:174
  239.1 3.3 %broadcast_multiply_fusion = f32[2,256,1024]{2,1,0:T(8,128)} fusion(f32[2,256,1024]{2,1,0:T(8,128)} %get-tuple-element.9), kind=kLoop, calls=%fused_computation.58 | loop fusion | flops 524288 | bytes 4194304 | tf_op jit(solution)/shard_map/div | solution.py:178
  (140 shorter events, 25.8 us)
Async XLA Ops:
  7.2 30.7 %copy-start = (bf16[4,128,1024]{2,1,0:T(8,128)(2,1)S(1)}, bf16[4,128,1024]{2,1,0:T(8,128)(2,1)}, u32[]{:S(2)}) copy-start(bf16[4,128,1024]{2,1,0:T(8,128)(2,1)} %param.31) | copy-start | bytes 3145732
  7.2 22.1 %copy-start.14 = (s32[128]{0:T(128)S(1)}, s32[128]{0:T(128)}, u32[]{:S(2)}) copy-start(s32[128]{0:T(128)} %param.22) | copy-start | bytes 1540
  7.2 18.8 %copy-start.9 = (bf16[256,256]{1,0:T(8,128)(2,1)S(1)}, bf16[256,256]{1,0:T(8,128)(2,1)}, u32[]{:S(2)}) copy-start(bf16[256,256]{1,0:T(8,128)(2,1)} %param.27) | copy-start | bytes 393220
  7.2 20.8 %copy-start.10 = (bf16[256,256]{1,0:T(8,128)(2,1)S(1)}, bf16[256,256]{1,0:T(8,128)(2,1)}, u32[]{:S(2)}) copy-start(bf16[256,256]{1,0:T(8,128)(2,1)} %param.28) | copy-start | bytes 393220
  7.2 24.6 %copy-start.12 = (s32[8,4]{0,1:T(4,128)S(1)}, s32[8,4]{0,1:T(4,128)}, u32[]{:S(2)}) copy-start(s32[8,4]{0,1:T(4,128)} %param.24) | copy-start | bytes 388
  7.2 25.3 %copy-start.1 = (s32[8]{0:T(128)S(1)}, s32[8]{0:T(128)}, u32[]{:S(2)}) copy-start(s32[8]{0:T(128)} %param.25) | copy-start | bytes 100
  7.2 27.3 %copy-start.11 = (bf16[256,256]{1,0:T(8,128)(2,1)S(1)}, bf16[256,256]{1,0:T(8,128)(2,1)}, u32[]{:S(2)}) copy-start(bf16[256,256]{1,0:T(8,128)(2,1)} %param.26) | copy-start | bytes 393220
  7.2 174.4 %all-reduce.5.cloned.1.call-start = ((), (), s32[]{:S(2)}) async-start(), calls=%async_computation | async-start | bytes 4718592 | tf_op jit(solution)/shard_map/psum | solution.py:175
  26.2 19.6 %collective-permute-start = (bf16[4,128,256]{2,1,0:T(8,128)(2,1)S(1)}, bf16[4,128,256]{2,1,0:T(8,128)(2,1)}, u32[]{:S(2)}, u32[]{:S(2)}) collective-permute-start(bf16[4,128,256]{2,1,0:T(8,128)(2,1)S(1)} %bitcast.196), channel_id=1, source_target_pairs={{12,0},{0,4},{4,8},{8,12},{13,1},{1,5},{5,9},{9,13},{14,2},{2,6},{... | collective-permute-start | bytes 786440 | tf_op jit(solution)/shard_map/ppermute | solution.py:17
  26.6 23.1 %collective-permute-start.2 = (bf16[4,128,256]{2,1,0:T(8,128)(2,1)S(1)}, bf16[4,128,256]{2,1,0:T(8,128)(2,1)}, u32[]{:S(2)}, u32[]{:S(2)}) collective-permute-start(bf16[4,128,256]{2,1,0:T(8,128)(2,1)S(1)} %bitcast.197), channel_id=1, source_target_pairs={{4,0},{8,4},{12,8},{0,12},{5,1},{9,5},{13,9},{1,13},{6,2},{10,6},{... | collective-permute-start | bytes 786440 | tf_op jit(solution)/shard_map/ppermute | solution.py:17
  28.3 31.7 %collective-permute-start.3 = (bf16[4,128,256]{2,1,0:T(8,128)(2,1)S(1)}, bf16[4,128,256]{2,1,0:T(8,128)(2,1)}, u32[]{:S(2)}, u32[]{:S(2)}) collective-permute-start(bf16[4,128,256]{2,1,0:T(8,128)(2,1)S(1)} %bitcast.194), channel_id=1, source_target_pairs={{4,0},{8,4},{12,8},{0,12},{5,1},{9,5},{13,9},{1,13},{6,2},{10,6},{... | collective-permute-start | bytes 786440 | tf_op jit(solution)/shard_map/ppermute | solution.py:17
  28.7 35.4 %collective-permute-start.1 = (bf16[4,128,256]{2,1,0:T(8,128)(2,1)S(1)}, bf16[4,128,256]{2,1,0:T(8,128)(2,1)}, u32[]{:S(2)}, u32[]{:S(2)}) collective-permute-start(bf16[4,128,256]{2,1,0:T(8,128)(2,1)S(1)} %bitcast.195), channel_id=1, source_target_pairs={{12,0},{0,4},{4,8},{8,12},{13,1},{1,5},{5,9},{9,13},{14,2},{2,6},{... | collective-permute-start | bytes 786440 | tf_op jit(solution)/shard_map/ppermute | solution.py:17
  50.8 2.9 %copy-start.2 = (f32[4,16,128,128]{3,2,1,0:T(8,128)S(1)}, f32[4,16,128,128]{3,2,1,0:T(8,128)}, u32[]{:S(2)}) copy-start(f32[4,16,128,128]{3,2,1,0:T(8,128)} %get-tuple-element.37) | copy-start | bytes 12582916
  50.8 5.0 %copy-start.3 = (f32[4,16,128,128]{3,2,1,0:T(8,128)S(1)}, f32[4,16,128,128]{3,2,1,0:T(8,128)}, u32[]{:S(2)}) copy-start(f32[4,16,128,128]{3,2,1,0:T(8,128)} %get-tuple-element.39) | copy-start | bytes 12582916
  51.8 6.3 %copy-start.4 = (f32[4,16,128,128]{3,2,1,0:T(8,128)}, f32[4,16,128,128]{3,2,1,0:T(8,128)S(1)}, u32[]{:S(2)}) copy-start(f32[4,16,128,128]{3,2,1,0:T(8,128)S(1)} %get-tuple-element.35) | copy-start | bytes 12582916
  55.8 2.3 copy-start.7
  65.3 3.6 %copy-start.13 = (bf16[256,256]{1,0:T(8,128)(2,1)S(1)}, bf16[256,256]{1,0:T(8,128)(2,1)}, u32[]{:S(2)}) copy-start(bf16[256,256]{1,0:T(8,128)(2,1)} %param.29) | copy-start | bytes 393220
  71.2 5.5 %copy-start.6 = (bf16[4,64,1024]{2,1,0:T(8,128)(2,1)S(1)}, bf16[4,64,1024]{2,1,0:T(8,128)(2,1)}, u32[]{:S(2)}) copy-start(bf16[4,64,1024]{2,1,0:T(8,128)(2,1)} %get-tuple-element.17) | copy-start | bytes 1572868
  78.8 0.8 copy-start.5
  84.0 155.2 %all-reduce.7.cloned.1.call-start = ((), (), s32[]{:S(2)}) async-start(), calls=%async_computation.1 | async-start | bytes 4718592 | tf_op jit(solution)/shard_map/psum | solution.py:174
  239.1 3.3 %copy-start.8 = (f32[256,256]{1,0:T(8,128)S(1)}, f32[256,256]{1,0:T(8,128)}, u32[]{:S(2)}) copy-start(f32[256,256]{1,0:T(8,128)} %get-tuple-element.10) | copy-start | bytes 786436
Sparse Core Ops, SparseCore 0:
  84.1 97.4 all-reduce.4
  184.1 54.9 all-reduce.6
